TPU v7x, 32 devices: a whole 2x2x4 slice. The times are simulated.
32 devices in a mesh: range: 16 (over z, y, x), chip: 2 (over core).
Axes of the slice: x: 2, y: 2, z: 4, core: 2. Of those that a mesh axis runs over, the one named last changes fastest.
Arguments:
- mode_tables: bfloat16 [32, 2048, 768], P('range', None, 'chip'), may hold values from -1 to 1
- attenuation: float32 [32, 768], P('range'), may hold values from 0 to 1, as said below
- excitation: float32 [768, 128], replicated, may hold values from -6 to 6
Outputs:
- fields: float32 [32, 2048, 128], P('range', 'chip')
Inputs may be any that keep to these rules, and one draw needn't show every extreme that they name: attenuation rates, positive.
All inputs are finite; a program needn't handle non-finite values.
Results may differ from a plain program's by a relative error of at most 0.0029.
Values may be sent and summed in bfloat16 or wider, within the bound.
A program may use at most 64 MiB of HBM per device.

v0:
```python
import jax
import jax.numpy as jnp
from jax import lax
from jax.sharding import PartitionSpec as P

highest = lax.Precision.HIGHEST


def from_behind(value, axis, steps):
    count = lax.axis_size(axis)
    initial, last = (max(0, -steps), min(count, count - steps))
    return lax.ppermute(value, axis, [(source, source + steps) for source in range(initial, last)])


def on_device(mode_tables, attenuation, excitation):
    seg_local, height_count, half_count = mode_tables.shape
    chip_count = lax.axis_size("chip")
    count_of_modes = half_count * chip_count
    range_count = lax.axis_size("range")
    position = lax.axis_index("range")
    core_index = lax.axis_index("chip")
    is_first = position == 0
    column_start = core_index * half_count
    identity = jnp.eye(count_of_modes, dtype=jnp.float32)
    damping = jnp.exp(-attenuation)
    earlier_half = from_behind(mode_tables[seg_local - 1], "range", 1)
    tables, earlier = (
        lax.all_gather(mode_tables, "chip", axis=2, tiled=True),
        lax.all_gather(earlier_half, "chip", axis=1, tiled=True),
    )
    previous = jnp.concatenate([earlier[None], tables[:-1]], axis=0)
    intersection = jnp.einsum("shm,shn->smn", tables, previous, preferred_element_type=jnp.float32)
    intersection = intersection.at[0].set(jnp.where(is_first, identity, intersection[0]))
    matrices = damping[:, :, None] * intersection
    prefix = lax.dynamic_slice_in_dim(matrices[0], column_start, half_count, 1)
    segment = 1
    prefix = jnp.dot(matrices[segment], prefix, precision=highest)
    rounds = (range_count - 1).bit_length()
    for level_index in range(rounds):
        distance = 2**level_index
        earlier_part = from_behind(prefix, "range", distance)
        product = jnp.dot(
            lax.all_gather(prefix, "chip", axis=1, tiled=True), earlier_part, precision=highest
        )
        prefix = jnp.where(position >= distance, product, prefix)
    source_rows = lax.dynamic_slice_in_dim(excitation, column_start, half_count, 0)
    reached = lax.psum(jnp.dot(prefix, source_rows, precision=highest), "chip")
    arriving = from_behind(reached, "range", 1)
    amplitude = jnp.where(is_first, excitation, arriving)
    stored = []
    segment = 0
    amplitude = jnp.dot(matrices[segment], amplitude, precision=highest)
    stored.append(amplitude.astype(jnp.bfloat16))
    stored.append(reached.astype(jnp.bfloat16))
    rounded = jnp.stack(stored)
    row_count = height_count // chip_count
    own_rows = lax.dynamic_slice_in_dim(tables, core_index * row_count, row_count, 1)
    return jnp.einsum("shm,smc->shc", own_rows, rounded, preferred_element_type=jnp.float32)


def solution(mesh):
    placed = (P("range", None, "chip"), P("range", None), P())
    return jax.shard_map(
        on_device, mesh=mesh, in_specs=placed, out_specs=P("range", "chip", None), check_vma=False
    )
```

profile of v0, /device:TPU:8, one launch (start us, length us, event | category | flops | bytes accessed | tf_op | source)
XLA Modules:
  0.0 304.3 jit_solution(1678558240698443344)
XLA Ops:
  6.5 0.7 all-gather.7.cloned.1.call-update
  7.3 1.1 copy-done.1
  8.4 0.2 slice_bitcast_fusion.2
  8.6 3.4 %collective-permute-start = (bf16[2048,384]{1,0:T(8,128)(2,1)S(1)}, bf16[2048,384]{1,0:T(8,128)(2,1)S(1)}, u32[]{:S(2)}, u32[]{:S(2)}) collective-permute-start(bf16[2048,384]{1,0:T(8,128)(2,1)S(1)} %slice_bitcast_fusion.2), channel_id=1, source_target_pairs={{0,2},{2,4},{4,6},{6,8},{8,10},{10,12},{12,14},{14,16},{16,18},{18... | collective-permute-start | bytes 4718600 | tf_op jit(solution)/shard_map/ppermute | solution.py:12
  12.0 36.4 %collective-permute-done = bf16[2048,384]{1,0:T(8,128)(2,1)S(1)} collective-permute-done((bf16[2048,384]{1,0:T(8,128)(2,1)S(1)}, bf16[2048,384]{1,0:T(8,128)(2,1)S(1)}, u32[]{:S(2)}, u32[]{:S(2)}) %collective-permute-start) | collective-permute-done | bytes 1572896 | tf_op jit(solution)/shard_map/ppermute | solution.py:12
  48.4 1.1 copy-done.2
  49.7 11.7 %all-gather.9.cloned.1.call-done = bf16[2048,768]{1,0:T(8,128)(2,1)} async-done(((bf16[2048,384]{1,0:T(8,128)(2,1)}), bf16[2048,768]{1,0:T(8,128)(2,1)}) %all-gather.9.cloned.1.call-update) | async-done | bytes 3145744 | tf_op jit(solution)/shard_map/all_gather | solution.py:29
  61.4 9.8 %fusion.10 = f32[2,768,768]{1,2,0:T(8,128)S(1)} fusion(bf16[2,2048,768]{2,1,0:T(8,128)(2,1)} %all-gather.7.cloned.1.call-done, bf16[1,2048,768]{2,1,0:T(8,128)(2,1)S(1)} %slice-done, bf16[1,2048,768]{2,1,0:T(8,128)(2,1)} %bitcast.32), kind=kOutput, calls=%fused_computation.14 | convolution fusion | flops 4834983936 | bytes 17301504 | tf_op jit(solution)/shard_map/shm,shn->smn/dot_general | solution.py:32
  71.2 0.4 fusion.7
  71.6 0.3 broadcast_multiply_fusion
  72.0 0.2 slice.43
  72.1 2.1 copy-done
  74.2 8.7 %fusion.6 = f32[768,384]{1,0:T(8,128)} fusion(f32[2,768,768]{1,2,0:T(8,128)S(1)} %broadcast_multiply_fusion, f32[1,768,768]{1,2,0:T(8,128)S(1)} %slice.43, s32[]{:T(128)S(6)} %select_n.58), kind=kOutput, calls=%fused_computation.7 | convolution fusion | flops 2717908992 | bytes 4718596 | tf_op jit(solution)/shard_map/dot_general | solution.py:37
  83.0 3.4 %collective-permute-start.1 = (f32[768,384]{1,0:T(8,128)}, f32[768,384]{1,0:T(8,128)S(1)}, u32[]{:S(2)}, u32[]{:S(2)}) collective-permute-start(f32[768,384]{1,0:T(8,128)} %fusion.6), channel_id=1, source_target_pairs={{0,2},{2,4},{4,6},{6,8},{8,10},{10,12},{12,14},{14,16},{16,18},{18... | collective-permute-start | bytes 3538952 | tf_op jit(solution)/shard_map/ppermute | solution.py:12
  86.4 28.7 %collective-permute-done.1 = f32[768,384]{1,0:T(8,128)S(1)} collective-permute-done((f32[768,384]{1,0:T(8,128)}, f32[768,384]{1,0:T(8,128)S(1)}, u32[]{:S(2)}, u32[]{:S(2)}) %collective-permute-start.1) | collective-permute-done | bytes 1179680 | tf_op jit(solution)/shard_map/ppermute | solution.py:12
  115.0 6.5 %convolution_select_fusion.3 = f32[768,384]{1,0:T(8,128)} fusion(f32[768,384]{1,0:T(8,128)} %fusion.6, f32[768,768]{1,0:T(8,128)} %all-gather.11.cloned.1.call-done, f32[768,384]{1,0:T(8,128)S(1)} %collective-permute-done.1, pred[]{:T(512)S(6)} %ge.15), kind=kOutput, calls=%fused_computation.19 | convolution fusion | flops 2718203904 | bytes 5898241 | tf_op jit(solution)/shard_map/dot_general | solution.py:42
  121.7 2.5 collective-permute-start.2
  124.2 27.8 %collective-permute-done.2 = f32[768,384]{1,0:T(8,128)S(1)} collective-permute-done((f32[768,384]{1,0:T(8,128)}, f32[768,384]{1,0:T(8,128)S(1)}, u32[]{:S(2)}, u32[]{:S(2)}) %collective-permute-start.2) | collective-permute-done | bytes 1179680 | tf_op jit(solution)/shard_map/ppermute | solution.py:12
  152.0 6.5 %convolution_select_fusion.2 = f32[768,384]{1,0:T(8,128)} fusion(f32[768,384]{1,0:T(8,128)} %convolution_select_fusion.3, f32[768,768]{1,0:T(8,128)} %all-gather.13.cloned.1.call-done, f32[768,384]{1,0:T(8,128)S(1)} %collective-permute-done.2, pred[]{:T(512)S(6)} %ge.14), kind=kOutput, calls=%fused_computation.18 | convolution fusion | flops 2718203904 | bytes 5898241 | tf_op jit(solution)/shard_map/dot_general | solution.py:42
  158.6 3.4 %collective-permute-start.3 = (f32[768,384]{1,0:T(8,128)}, f32[768,384]{1,0:T(8,128)S(1)}, u32[]{:S(2)}, u32[]{:S(2)}) collective-permute-start(f32[768,384]{1,0:T(8,128)} %convolution_select_fusion.2), channel_id=1, source_target_pairs={{0,8},{2,10},{4,12},{6,14},{8,16},{10,18},{12,20},{14,22},{16,24},... | collective-permute-start | bytes 3538952 | tf_op jit(solution)/shard_map/ppermute | solution.py:12
  162.0 25.2 %collective-permute-done.3 = f32[768,384]{1,0:T(8,128)S(1)} collective-permute-done((f32[768,384]{1,0:T(8,128)}, f32[768,384]{1,0:T(8,128)S(1)}, u32[]{:S(2)}, u32[]{:S(2)}) %collective-permute-start.3) | collective-permute-done | bytes 1179680 | tf_op jit(solution)/shard_map/ppermute | solution.py:12
  187.1 6.5 %convolution_select_fusion.1 = f32[768,384]{1,0:T(8,128)} fusion(f32[768,384]{1,0:T(8,128)} %convolution_select_fusion.2, f32[768,768]{1,0:T(8,128)} %all-gather.15.cloned.1.call-done, f32[768,384]{1,0:T(8,128)S(1)} %collective-permute-done.3, pred[]{:T(512)S(6)} %ge.13), kind=kOutput, calls=%fused_computation.17 | convolution fusion | flops 2718203904 | bytes 5898241 | tf_op jit(solution)/shard_map/dot_general | solution.py:42
  193.8 4.6 %collective-permute-start.4 = (f32[768,384]{1,0:T(8,128)}, f32[768,384]{1,0:T(8,128)S(1)}, u32[]{:S(2)}, u32[]{:S(2)}) collective-permute-start(f32[768,384]{1,0:T(8,128)} %convolution_select_fusion.1), channel_id=1, source_target_pairs={{0,16},{2,18},{4,20},{6,22},{8,24},{10,26},{12,28},{14,30},{1,17},... | collective-permute-start | bytes 3538952 | tf_op jit(solution)/shard_map/ppermute | solution.py:12
  198.4 48.4 %collective-permute-done.4 = f32[768,384]{1,0:T(8,128)S(1)} collective-permute-done((f32[768,384]{1,0:T(8,128)}, f32[768,384]{1,0:T(8,128)S(1)}, u32[]{:S(2)}, u32[]{:S(2)}) %collective-permute-start.4) | collective-permute-done | bytes 1179680 | tf_op jit(solution)/shard_map/ppermute | solution.py:12
  246.7 5.8 %convolution_select_fusion = f32[768,384]{1,0:T(8,128)S(1)} fusion(f32[768,384]{1,0:T(8,128)} %convolution_select_fusion.1, f32[768,768]{1,0:T(8,128)} %all-gather.17.cloned.1.call-done, f32[768,384]{1,0:T(8,128)S(1)} %collective-permute-done.4, pred[]{:T(512)S(6)} %ge.12), kind=kOutput, calls=%fused_computation.16 | convolution fusion | flops 2718203904 | bytes 5898241 | tf_op jit(solution)/shard_map/dot_general | solution.py:42
  252.6 1.9 fusion.25
  254.5 18.5 %all-reduce.2.cloned.1.call-done = f32[768,128]{1,0:T(8,128)} async-done(((f32[768,128]{1,0:T(8,128)}), f32[768,128]{1,0:T(8,128)}) %all-reduce.2.cloned.1.call-update) | async-done | bytes 393232 | tf_op jit(solution)/shard_map/psum | solution.py:47
  273.0 3.4 %collective-permute-start.5 = (f32[768,128]{1,0:T(8,128)}, f32[768,128]{1,0:T(8,128)S(1)}, u32[]{:S(2)}, u32[]{:S(2)}) collective-permute-start(f32[768,128]{1,0:T(8,128)} %all-reduce.2.cloned.1.call-done), channel_id=1, source_target_pairs={{0,2},{2,4},{4,6},{6,8},{8,10},{10,12},{12,14},{14,16},{16,18},{18... | collective-permute-start | bytes 1179656 | tf_op jit(solution)/shard_map/ppermute | solution.py:12
  276.4 1.0 convert_bitcast_fusion
  277.4 10.8 %collective-permute-done.5 = f32[768,128]{1,0:T(8,128)S(1)} collective-permute-done((f32[768,128]{1,0:T(8,128)}, f32[768,128]{1,0:T(8,128)S(1)}, u32[]{:S(2)}, u32[]{:S(2)}) %collective-permute-start.5) | collective-permute-done | bytes 393248 | tf_op jit(solution)/shard_map/ppermute | solution.py:12
  288.2 5.5 %fusion.18 = bf16[1,768,128]{2,1,0:T(8,128)(2,1)S(1)} fusion(f32[768,128]{1,0:T(8,128)S(1)} %copy-done.3, f32[768,128]{1,0:T(8,128)S(1)} %collective-permute-done.5, pred[]{:T(512)S(6)} %eq.11, f32[2,768,768]{1,2,0:T(8,128)} %copy-done), kind=kOutput, calls=%fused_computation.23 | convolution fusion | flops 906166272 | bytes 3342337 | tf_op jit(solution)/shard_map/dot_general | solution.py:52
  293.6 3.9 %fusion.4 = f32[2,1024,128]{2,1,0:T(8,128)} fusion(bf16[2,2048,768]{2,1,0:T(8,128)(2,1)} %all-gather.7.cloned.1.call-done, s32[]{:T(128)S(6)} %select_n.50, bf16[1,768,128]{2,1,0:T(8,128)(2,1)S(1)} %convert_bitcast_fusion, bf16[1,768,128]{2,1,0:T(8,128)(2,1)S(1)} %fusion.18), kind=kOutput, calls=%fused_computation.4 | convolution fusion | flops 402849792 | bytes 4587524 | tf_op jit(solution)/shard_map/shm,smc->shc/dot_general | solution.py:58
  (28 shorter events, 0.4 us)
Async XLA Ops:
  6.5 1.9 copy-start.1
  6.5 43.2 %all-gather.7.cloned.1.call-start = ((), (), s32[]{:S(2)}) async-start(), calls=%async_computation | async-start | bytes 9437184 | tf_op jit(solution)/shard_map/all_gather | solution.py:28
  7.3 42.4 %copy-start.4 = (f32[2,768]{1,0:T(2,128)S(1)}, f32[2,768]{1,0:T(2,128)}, u32[]{:S(2)}) copy-start(f32[2,768]{1,0:T(2,128)} %param.6) | copy-start | bytes 18436
  7.3 54.1 %all-gather.9.cloned.1.call-start = ((), (), s32[]{:S(2)}) async-start(), calls=%async_computation.1 | async-start | bytes 4718592 | tf_op jit(solution)/shard_map/all_gather | solution.py:29
  8.6 39.8 %collective-permute-start = (bf16[2048,384]{1,0:T(8,128)(2,1)S(1)}, bf16[2048,384]{1,0:T(8,128)(2,1)S(1)}, u32[]{:S(2)}, u32[]{:S(2)}) collective-permute-start(bf16[2048,384]{1,0:T(8,128)(2,1)S(1)} %slice_bitcast_fusion.2), channel_id=1, source_target_pairs={{0,2},{2,4},{4,6},{6,8},{8,10},{10,12},{12,14},{14,16},{16,18},{18... | collective-permute-start | bytes 4718600 | tf_op jit(solution)/shard_map/ppermute | solution.py:12
  48.4 1.1 copy-start.2
  49.6 65.4 %all-gather.11.cloned.1.call-start = ((), (), s32[]{:S(2)}) async-start(), calls=%async_computation.2 | async-start | bytes 3538944 | tf_op jit(solution)/shard_map/all_gather | solution.py:43
  49.7 11.7 %slice-start = ((bf16[2,2048,768]{2,1,0:T(8,128)(2,1)}), bf16[1,2048,768]{2,1,0:T(8,128)(2,1)S(1)}, s32[]{:S(2)}) async-start(bf16[2,2048,768]{2,1,0:T(8,128)(2,1)} %all-gather.7.cloned.1.call-done), calls=%async_computation.7 | async-start | bytes 6291456 | tf_op jit(solution)/shard_map/slice | solution.py:31
  71.9 2.2 copy-start
  82.9 69.0 %all-gather.13.cloned.1.call-start = ((), (), s32[]{:S(2)}) async-start(), calls=%async_computation.3 | async-start | bytes 3538944 | tf_op jit(solution)/shard_map/all_gather | solution.py:43
  83.0 32.1 %collective-permute-start.1 = (f32[768,384]{1,0:T(8,128)}, f32[768,384]{1,0:T(8,128)S(1)}, u32[]{:S(2)}, u32[]{:S(2)}) collective-permute-start(f32[768,384]{1,0:T(8,128)} %fusion.6), channel_id=1, source_target_pairs={{0,2},{2,4},{4,6},{6,8},{8,10},{10,12},{12,14},{14,16},{16,18},{18... | collective-permute-start | bytes 3538952 | tf_op jit(solution)/shard_map/ppermute | solution.py:12
  121.6 65.5 %all-gather.15.cloned.1.call-start = ((), (), s32[]{:S(2)}) async-start(), calls=%async_computation.4 | async-start | bytes 3538944 | tf_op jit(solution)/shard_map/all_gather | solution.py:43
  121.7 30.3 %collective-permute-start.2 = (f32[768,384]{1,0:T(8,128)}, f32[768,384]{1,0:T(8,128)S(1)}, u32[]{:S(2)}, u32[]{:S(2)}) collective-permute-start(f32[768,384]{1,0:T(8,128)} %convolution_select_fusion.3), channel_id=1, source_target_pairs={{0,4},{2,6},{4,8},{6,10},{8,12},{10,14},{12,16},{14,18},{16,20},{1... | collective-permute-start | bytes 3538952 | tf_op jit(solution)/shard_map/ppermute | solution.py:12
  158.5 88.2 %all-gather.17.cloned.1.call-start = ((), (), s32[]{:S(2)}) async-start(), calls=%async_computation.5 | async-start | bytes 3538944 | tf_op jit(solution)/shard_map/all_gather | solution.py:43
  158.6 28.6 %collective-permute-start.3 = (f32[768,384]{1,0:T(8,128)}, f32[768,384]{1,0:T(8,128)S(1)}, u32[]{:S(2)}, u32[]{:S(2)}) collective-permute-start(f32[768,384]{1,0:T(8,128)} %convolution_select_fusion.2), channel_id=1, source_target_pairs={{0,8},{2,10},{4,12},{6,14},{8,16},{10,18},{12,20},{14,22},{16,24},... | collective-permute-start | bytes 3538952 | tf_op jit(solution)/shard_map/ppermute | solution.py:12
  193.7 79.3 %all-reduce.2.cloned.1.call-start = ((), (), s32[]{:S(2)}) async-start(), calls=%async_computation.6 | async-start | bytes 786432 | tf_op jit(solution)/shard_map/psum | solution.py:47
  193.8 53.0 %collective-permute-start.4 = (f32[768,384]{1,0:T(8,128)}, f32[768,384]{1,0:T(8,128)S(1)}, u32[]{:S(2)}, u32[]{:S(2)}) collective-permute-start(f32[768,384]{1,0:T(8,128)} %convolution_select_fusion.1), channel_id=1, source_target_pairs={{0,16},{2,18},{4,20},{6,22},{8,24},{10,26},{12,28},{14,30},{1,17},... | collective-permute-start | bytes 3538952 | tf_op jit(solution)/shard_map/ppermute | solution.py:12
  198.3 54.2 %copy-start.3 = (f32[768,128]{1,0:T(8,128)S(1)}, f32[768,128]{1,0:T(8,128)}, u32[]{:S(2)}) copy-start(f32[768,128]{1,0:T(8,128)} %param.7) | copy-start | bytes 1179652
  273.0 15.2 %collective-permute-start.5 = (f32[768,128]{1,0:T(8,128)}, f32[768,128]{1,0:T(8,128)S(1)}, u32[]{:S(2)}, u32[]{:S(2)}) collective-permute-start(f32[768,128]{1,0:T(8,128)} %all-reduce.2.cloned.1.call-done), channel_id=1, source_target_pairs={{0,2},{2,4},{4,6},{6,8},{8,10},{10,12},{12,14},{14,16},{16,18},{18... | collective-permute-start | bytes 1179656 | tf_op jit(solution)/shard_map/ppermute | solution.py:12
Sparse Core Ops, SparseCore 0:
  8.9 17.9 all-gather.6
  49.7 11.6 all-gather.8
  83.0 12.1 all-gather.10
  121.7 10.3 all-gather.12
  158.7 10.2 all-gather.14
  193.8 10.2 all-gather.16
  254.6 18.3 all-reduce.1
where the time goes:
time: 305 us; the launch traced here: 304 us
  waiting for transfers between devices  208 us (68%)
  matrix products  55.2 us (18%)
  starting transfers between devices  20.8 us (7%)
  between operations  13.7 us (4%)
  local copies, waits for them, and re-layouts  4.66 us (2%)
    ppermute x6, waiting for transfers between devices, from_behind(): lax.ppermute(value, axis, [(source, source + steps) for source in range(i...  177 us
    dot_general x4, matrix products, on_device(): jnp.dot(lax.all_gather(prefix, 'chip', axis=1, tiled=True), earlier_part,...  25.5 us
    ppermute x6, starting transfers between devices, from_behind(): lax.ppermute(value, axis, [(source, source + steps) for source in range(i...  20.6 us
    psum x1, waiting for transfers between devices, on_device(): reached = lax.psum(jnp.dot(prefix, source_rows, precision=highest), 'chip')  18.5 us
    all_gather x1, waiting for transfers between devices, on_device(): lax.all_gather(earlier_half, 'chip', axis=1, tiled=True)  11.7 us
    dot_general x1, matrix products, on_device(): jnp.einsum('shm,shn->smn', tables, previous, preferred_element_type=jnp.f...  9.84 us
    dot_general x1, matrix products, on_device(): prefix = jnp.dot(matrices[segment], prefix, precision=highest)  8.7 us
  transfers between devices with their start and end apart: 13, of which 8 were waited for; matrix products, arithmetic and copies ran while one was open for 0% of the time, Pallas kernels for 0%

commit v1 on v0

--- a/solution.py
+++ b/solution.py
@@ -44,7 +44,9 @@
         )
         prefix = jnp.where(position >= distance, product, prefix)
     source_rows = lax.dynamic_slice_in_dim(excitation, column_start, half_count, 0)
-    reached = lax.psum(jnp.dot(prefix, source_rows, precision=highest), "chip")
+    reached = jnp.sum(
+        lax.all_gather(jnp.dot(prefix, source_rows, precision=highest), "chip"), axis=0
+    )
     arriving = from_behind(reached, "range", 1)
     amplitude = jnp.where(is_first, excitation, arriving)
     stored = []

time: 305 us -> 288 us (0.944)
  waiting for transfers between devices: 208 us -> 192 us
    psum x1 -> x0, waiting for transfers between devices: 18.5 us -> none  [on_device(): reached = lax.psum(jnp.dot(prefix, source_rows, precision=highest), 'chip')]
  transfers between devices with their start and end apart: 13 -> 12, of which waited for: 8 -> 7; matrix products, arithmetic and copies ran while one was open for 0% -> 0% of each run, Pallas kernels for 0% -> 0%
where the time goes in v1:
time: 288 us; the launch traced here: 287 us
  waiting for transfers between devices  192 us (67%)
  matrix products  54.5 us (19%)
  starting transfers between devices  19.4 us (7%)
  between operations  13.7 us (5%)
  local copies, waits for them, and re-layouts  4.65 us (2%)
    ppermute x6, waiting for transfers between devices, from_behind(): lax.ppermute(value, axis, [(source, source + steps) for source in range(i...  179 us
    dot_general x4, matrix products, on_device(): jnp.dot(lax.all_gather(prefix, 'chip', axis=1, tiled=True), earlier_part,...  25.5 us
    ppermute x6, starting transfers between devices, from_behind(): lax.ppermute(value, axis, [(source, source + steps) for source in range(i...  19.2 us
    all_gather x1, waiting for transfers between devices, on_device(): lax.all_gather(earlier_half, 'chip', axis=1, tiled=True)  11.7 us
    dot_general x1, matrix products, on_device(): jnp.einsum('shm,shn->smn', tables, previous, preferred_element_type=jnp.f...  9.85 us
    dot_general x1, matrix products, on_device(): prefix = jnp.dot(matrices[segment], prefix, precision=highest)  8.7 us
  transfers between devices with their start and end apart: 12, of which 7 were waited for; matrix products, arithmetic and copies ran while one was open for 0% of the time, Pallas kernels for 0%

profile of v1, /device:TPU:8, one launch (start us, length us, event | category | flops | bytes accessed | tf_op | source)
XLA Modules:
  0.0 287.2 jit_solution(5376696231832216865)
XLA Ops:
  6.5 0.7 all-gather.8.cloned.1.call-update
  7.3 1.1 copy-done.1
  8.4 0.2 slice_bitcast_fusion.2
  8.6 3.4 %collective-permute-start = (bf16[2048,384]{1,0:T(8,128)(2,1)S(1)}, bf16[2048,384]{1,0:T(8,128)(2,1)S(1)}, u32[]{:S(2)}, u32[]{:S(2)}) collective-permute-start(bf16[2048,384]{1,0:T(8,128)(2,1)S(1)} %slice_bitcast_fusion.2), channel_id=1, source_target_pairs={{0,2},{2,4},{4,6},{6,8},{8,10},{10,12},{12,14},{14,16},{16,18},{18... | collective-permute-start | bytes 4718600 | tf_op jit(solution)/shard_map/ppermute | solution.py:12
  12.0 36.4 %collective-permute-done = bf16[2048,384]{1,0:T(8,128)(2,1)S(1)} collective-permute-done((bf16[2048,384]{1,0:T(8,128)(2,1)S(1)}, bf16[2048,384]{1,0:T(8,128)(2,1)S(1)}, u32[]{:S(2)}, u32[]{:S(2)}) %collective-permute-start) | collective-permute-done | bytes 1572896 | tf_op jit(solution)/shard_map/ppermute | solution.py:12
  48.4 1.1 copy-done.2
  49.7 11.7 %all-gather.10.cloned.1.call-done = bf16[2048,768]{1,0:T(8,128)(2,1)} async-done(((bf16[2048,384]{1,0:T(8,128)(2,1)}), bf16[2048,768]{1,0:T(8,128)(2,1)}) %all-gather.10.cloned.1.call-update) | async-done | bytes 3145744 | tf_op jit(solution)/shard_map/all_gather | solution.py:29
  61.4 9.8 %fusion.10 = f32[2,768,768]{1,2,0:T(8,128)S(1)} fusion(bf16[2,2048,768]{2,1,0:T(8,128)(2,1)} %all-gather.8.cloned.1.call-done, bf16[1,2048,768]{2,1,0:T(8,128)(2,1)S(1)} %slice-done, bf16[1,2048,768]{2,1,0:T(8,128)(2,1)} %bitcast.34), kind=kOutput, calls=%fused_computation.14 | convolution fusion | flops 4834983936 | bytes 17301504 | tf_op jit(solution)/shard_map/shm,shn->smn/dot_general | solution.py:32
  71.2 0.4 fusion.7
  71.6 0.3 broadcast_multiply_fusion
  72.0 0.2 slice.43
  72.1 2.1 copy-done
  74.2 8.7 %fusion.6 = f32[768,384]{1,0:T(8,128)} fusion(f32[2,768,768]{1,2,0:T(8,128)S(1)} %broadcast_multiply_fusion, f32[1,768,768]{1,2,0:T(8,128)S(1)} %slice.43, s32[]{:T(128)S(6)} %select_n.58), kind=kOutput, calls=%fused_computation.7 | convolution fusion | flops 2717908992 | bytes 4718596 | tf_op jit(solution)/shard_map/dot_general | solution.py:37
  83.0 3.4 %collective-permute-start.1 = (f32[768,384]{1,0:T(8,128)}, f32[768,384]{1,0:T(8,128)S(1)}, u32[]{:S(2)}, u32[]{:S(2)}) collective-permute-start(f32[768,384]{1,0:T(8,128)} %fusion.6), channel_id=1, source_target_pairs={{0,2},{2,4},{4,6},{6,8},{8,10},{10,12},{12,14},{14,16},{16,18},{18... | collective-permute-start | bytes 3538952 | tf_op jit(solution)/shard_map/ppermute | solution.py:12
  86.3 28.7 %collective-permute-done.1 = f32[768,384]{1,0:T(8,128)S(1)} collective-permute-done((f32[768,384]{1,0:T(8,128)}, f32[768,384]{1,0:T(8,128)S(1)}, u32[]{:S(2)}, u32[]{:S(2)}) %collective-permute-start.1) | collective-permute-done | bytes 1179680 | tf_op jit(solution)/shard_map/ppermute | solution.py:12
  115.0 6.5 %convolution_select_fusion.3 = f32[768,384]{1,0:T(8,128)} fusion(f32[768,384]{1,0:T(8,128)} %fusion.6, f32[768,768]{1,0:T(8,128)} %all-gather.12.cloned.1.call-done, f32[768,384]{1,0:T(8,128)S(1)} %collective-permute-done.1, pred[]{:T(512)S(6)} %ge.15), kind=kOutput, calls=%fused_computation.19 | convolution fusion | flops 2718203904 | bytes 5898241 | tf_op jit(solution)/shard_map/dot_general | solution.py:42
  121.6 2.5 collective-permute-start.2
  124.1 27.8 %collective-permute-done.2 = f32[768,384]{1,0:T(8,128)S(1)} collective-permute-done((f32[768,384]{1,0:T(8,128)}, f32[768,384]{1,0:T(8,128)S(1)}, u32[]{:S(2)}, u32[]{:S(2)}) %collective-permute-start.2) | collective-permute-done | bytes 1179680 | tf_op jit(solution)/shard_map/ppermute | solution.py:12
  151.9 6.5 %convolution_select_fusion.2 = f32[768,384]{1,0:T(8,128)} fusion(f32[768,384]{1,0:T(8,128)} %convolution_select_fusion.3, f32[768,768]{1,0:T(8,128)} %all-gather.14.cloned.1.call-done, f32[768,384]{1,0:T(8,128)S(1)} %collective-permute-done.2, pred[]{:T(512)S(6)} %ge.14), kind=kOutput, calls=%fused_computation.18 | convolution fusion | flops 2718203904 | bytes 5898241 | tf_op jit(solution)/shard_map/dot_general | solution.py:42
  158.6 3.4 %collective-permute-start.3 = (f32[768,384]{1,0:T(8,128)}, f32[768,384]{1,0:T(8,128)S(1)}, u32[]{:S(2)}, u32[]{:S(2)}) collective-permute-start(f32[768,384]{1,0:T(8,128)} %convolution_select_fusion.2), channel_id=1, source_target_pairs={{0,8},{2,10},{4,12},{6,14},{8,16},{10,18},{12,20},{14,22},{16,24},... | collective-permute-start | bytes 3538952 | tf_op jit(solution)/shard_map/ppermute | solution.py:12
  162.0 25.1 %collective-permute-done.3 = f32[768,384]{1,0:T(8,128)S(1)} collective-permute-done((f32[768,384]{1,0:T(8,128)}, f32[768,384]{1,0:T(8,128)S(1)}, u32[]{:S(2)}, u32[]{:S(2)}) %collective-permute-start.3) | collective-permute-done | bytes 1179680 | tf_op jit(solution)/shard_map/ppermute | solution.py:12
  187.1 6.5 %convolution_select_fusion.1 = f32[768,384]{1,0:T(8,128)} fusion(f32[768,384]{1,0:T(8,128)} %convolution_select_fusion.2, f32[768,768]{1,0:T(8,128)} %all-gather.16.cloned.1.call-done, f32[768,384]{1,0:T(8,128)S(1)} %collective-permute-done.3, pred[]{:T(512)S(6)} %ge.13), kind=kOutput, calls=%fused_computation.17 | convolution fusion | flops 2718203904 | bytes 5898241 | tf_op jit(solution)/shard_map/dot_general | solution.py:42
  193.7 4.6 %collective-permute-start.4 = (f32[768,384]{1,0:T(8,128)}, f32[768,384]{1,0:T(8,128)S(1)}, u32[]{:S(2)}, u32[]{:S(2)}) collective-permute-start(f32[768,384]{1,0:T(8,128)} %convolution_select_fusion.1), channel_id=1, source_target_pairs={{0,16},{2,18},{4,20},{6,22},{8,24},{10,26},{12,28},{14,30},{1,17},... | collective-permute-start | bytes 3538952 | tf_op jit(solution)/shard_map/ppermute | solution.py:12
  198.3 48.4 %collective-permute-done.4 = f32[768,384]{1,0:T(8,128)S(1)} collective-permute-done((f32[768,384]{1,0:T(8,128)}, f32[768,384]{1,0:T(8,128)S(1)}, u32[]{:S(2)}, u32[]{:S(2)}) %collective-permute-start.4) | collective-permute-done | bytes 1179680 | tf_op jit(solution)/shard_map/ppermute | solution.py:12
  246.7 5.8 %convolution_select_fusion = f32[768,384]{1,0:T(8,128)S(1)} fusion(f32[768,384]{1,0:T(8,128)} %convolution_select_fusion.1, f32[768,768]{1,0:T(8,128)} %all-gather.18.cloned.1.call-done, f32[768,384]{1,0:T(8,128)S(1)} %collective-permute-done.4, pred[]{:T(512)S(6)} %ge.12), kind=kOutput, calls=%fused_computation.16 | convolution fusion | flops 2718203904 | bytes 5898241 | tf_op jit(solution)/shard_map/dot_general | solution.py:42
  252.5 1.2 fusion.25
  253.7 2.4 all-gather
  256.1 0.1 reduce_sum.9
  256.2 1.9 collective-permute-start.5
  258.1 12.9 %collective-permute-done.5 = f32[768,128]{1,0:T(8,128)S(1)} collective-permute-done((f32[768,128]{1,0:T(8,128)S(1)}, f32[768,128]{1,0:T(8,128)S(1)}, u32[]{:S(2)}, u32[]{:S(2)}) %collective-permute-start.5) | collective-permute-done | bytes 393248 | tf_op jit(solution)/shard_map/ppermute | solution.py:12
  271.0 5.5 %fusion.18 = bf16[1,768,128]{2,1,0:T(8,128)(2,1)S(1)} fusion(f32[768,128]{1,0:T(8,128)S(1)} %copy-done.3, f32[768,128]{1,0:T(8,128)S(1)} %collective-permute-done.5, pred[]{:T(512)S(6)} %eq.11, f32[2,768,768]{1,2,0:T(8,128)} %copy-done), kind=kOutput, calls=%fused_computation.23 | convolution fusion | flops 906166272 | bytes 3342337 | tf_op jit(solution)/shard_map/dot_general | solution.py:54
  276.5 3.9 %fusion.4 = f32[2,1024,128]{2,1,0:T(8,128)} fusion(bf16[2,2048,768]{2,1,0:T(8,128)(2,1)} %all-gather.8.cloned.1.call-done, s32[]{:T(128)S(6)} %select_n.50, bf16[1,768,128]{2,1,0:T(8,128)(2,1)S(1)} %convert_bitcast_fusion, bf16[1,768,128]{2,1,0:T(8,128)(2,1)S(1)} %fusion.18), kind=kOutput, calls=%fused_computation.4 | convolution fusion | flops 402849792 | bytes 4587524 | tf_op jit(solution)/shard_map/shm,smc->shc/dot_general | solution.py:60
  (27 shorter events, 0.4 us)
Async XLA Ops:
  6.5 1.9 copy-start.1
  6.5 43.2 %all-gather.8.cloned.1.call-start = ((), (), s32[]{:S(2)}) async-start(), calls=%async_computation | async-start | bytes 9437184 | tf_op jit(solution)/shard_map/all_gather | solution.py:28
  7.3 42.4 %copy-start.4 = (f32[2,768]{1,0:T(2,128)S(1)}, f32[2,768]{1,0:T(2,128)}, u32[]{:S(2)}) copy-start(f32[2,768]{1,0:T(2,128)} %param.6) | copy-start | bytes 18436
  7.3 54.1 %all-gather.10.cloned.1.call-start = ((), (), s32[]{:S(2)}) async-start(), calls=%async_computation.1 | async-start | bytes 4718592 | tf_op jit(solution)/shard_map/all_gather | solution.py:29
  8.6 39.8 %collective-permute-start = (bf16[2048,384]{1,0:T(8,128)(2,1)S(1)}, bf16[2048,384]{1,0:T(8,128)(2,1)S(1)}, u32[]{:S(2)}, u32[]{:S(2)}) collective-permute-start(bf16[2048,384]{1,0:T(8,128)(2,1)S(1)} %slice_bitcast_fusion.2), channel_id=1, source_target_pairs={{0,2},{2,4},{4,6},{6,8},{8,10},{10,12},{12,14},{14,16},{16,18},{18... | collective-permute-start | bytes 4718600 | tf_op jit(solution)/shard_map/ppermute | solution.py:12
  48.4 1.1 copy-start.2
  49.6 65.4 %all-gather.12.cloned.1.call-start = ((), (), s32[]{:S(2)}) async-start(), calls=%async_computation.2 | async-start | bytes 3538944 | tf_op jit(solution)/shard_map/all_gather | solution.py:43
  49.7 11.7 %slice-start = ((bf16[2,2048,768]{2,1,0:T(8,128)(2,1)}), bf16[1,2048,768]{2,1,0:T(8,128)(2,1)S(1)}, s32[]{:S(2)}) async-start(bf16[2,2048,768]{2,1,0:T(8,128)(2,1)} %all-gather.8.cloned.1.call-done), calls=%async_computation.6 | async-start | bytes 6291456 | tf_op jit(solution)/shard_map/slice | solution.py:31
  71.9 2.2 copy-start
  82.9 69.0 %all-gather.14.cloned.1.call-start = ((), (), s32[]{:S(2)}) async-start(), calls=%async_computation.3 | async-start | bytes 3538944 | tf_op jit(solution)/shard_map/all_gather | solution.py:43
  83.0 32.1 %collective-permute-start.1 = (f32[768,384]{1,0:T(8,128)}, f32[768,384]{1,0:T(8,128)S(1)}, u32[]{:S(2)}, u32[]{:S(2)}) collective-permute-start(f32[768,384]{1,0:T(8,128)} %fusion.6), channel_id=1, source_target_pairs={{0,2},{2,4},{4,6},{6,8},{8,10},{10,12},{12,14},{14,16},{16,18},{18... | collective-permute-start | bytes 3538952 | tf_op jit(solution)/shard_map/ppermute | solution.py:12
  121.6 65.5 %all-gather.16.cloned.1.call-start = ((), (), s32[]{:S(2)}) async-start(), calls=%async_computation.4 | async-start | bytes 3538944 | tf_op jit(solution)/shard_map/all_gather | solution.py:43
  121.6 30.3 %collective-permute-start.2 = (f32[768,384]{1,0:T(8,128)}, f32[768,384]{1,0:T(8,128)S(1)}, u32[]{:S(2)}, u32[]{:S(2)}) collective-permute-start(f32[768,384]{1,0:T(8,128)} %convolution_select_fusion.3), channel_id=1, source_target_pairs={{0,4},{2,6},{4,8},{6,10},{8,12},{10,14},{12,16},{14,18},{16,20},{1... | collective-permute-start | bytes 3538952 | tf_op jit(solution)/shard_map/ppermute | solution.py:12
  158.5 88.2 %all-gather.18.cloned.1.call-start = ((), (), s32[]{:S(2)}) async-start(), calls=%async_computation.5 | async-start | bytes 3538944 | tf_op jit(solution)/shard_map/all_gather | solution.py:43
  158.6 28.6 %collective-permute-start.3 = (f32[768,384]{1,0:T(8,128)}, f32[768,384]{1,0:T(8,128)S(1)}, u32[]{:S(2)}, u32[]{:S(2)}) collective-permute-start(f32[768,384]{1,0:T(8,128)} %convolution_select_fusion.2), channel_id=1, source_target_pairs={{0,8},{2,10},{4,12},{6,14},{8,16},{10,18},{12,20},{14,22},{16,24},... | collective-permute-start | bytes 3538952 | tf_op jit(solution)/shard_map/ppermute | solution.py:12
  193.7 53.0 %collective-permute-start.4 = (f32[768,384]{1,0:T(8,128)}, f32[768,384]{1,0:T(8,128)S(1)}, u32[]{:S(2)}, u32[]{:S(2)}) collective-permute-start(f32[768,384]{1,0:T(8,128)} %convolution_select_fusion.1), channel_id=1, source_target_pairs={{0,16},{2,18},{4,20},{6,22},{8,24},{10,26},{12,28},{14,30},{1,17},... | collective-permute-start | bytes 3538952 | tf_op jit(solution)/shard_map/ppermute | solution.py:12
  198.3 54.2 %copy-start.3 = (f32[768,128]{1,0:T(8,128)S(1)}, f32[768,128]{1,0:T(8,128)}, u32[]{:S(2)}) copy-start(f32[768,128]{1,0:T(8,128)} %param.7) | copy-start | bytes 1179652
  256.2 14.8 %collective-permute-start.5 = (f32[768,128]{1,0:T(8,128)S(1)}, f32[768,128]{1,0:T(8,128)S(1)}, u32[]{:S(2)}, u32[]{:S(2)}) collective-permute-start(f32[768,128]{1,0:T(8,128)S(1)} %reduce_sum.9), channel_id=1, source_target_pairs={{0,2},{2,4},{4,6},{6,8},{8,10},{10,12},{12,14},{14,16},{16,18},{18... | collective-permute-start | bytes 1179656 | tf_op jit(solution)/shard_map/ppermute | solution.py:12
Sparse Core Ops, SparseCore 0:
  8.9 17.9 all-gather.7
  49.7 11.6 all-gather.9
  83.0 12.1 all-gather.11
  121.7 10.3 all-gather.13
  158.6 10.3 all-gather.15
  193.8 10.3 all-gather.17
